TPU v7x, 32 devices: a whole 2x2x4 slice. The times are simulated.
32 devices in a mesh: parts: 2 (over y), off: 4 (over z), depth: 2 (over x), shot: 2 (over core).
Axes of the slice: x: 2, y: 2, z: 4, core: 2. Of those that a mesh axis runs over, the one named last changes fastest.
Arguments:
- image: bfloat16 [64, 32, 32, 256], P('off', None, 'depth'), may hold values from -4 to 4
- offset_of: int32 [64], P('off'), may hold values from 0 to 63, each once
- background: bfloat16 [4, 32, 32, 256], P(('parts', 'shot'), 'off', 'depth'), parts along dimension 0, may hold values from -6 to 6
- wave_now: float32 [4, 32, 32, 256], P(('parts', 'shot'), 'off', 'depth'), parts along dimension 0, may hold values from -6 to 6
- wave_prev: float32 [4, 32, 32, 256], P(('parts', 'shot'), 'off', 'depth'), parts along dimension 0, may hold values from -6 to 6
- courant: float32 [32, 32, 256], P('off', 'depth'), may hold values from 0.02 to 0.15
Outputs:
- wave_next: float32 [4, 32, 32, 256], P(('parts', 'shot'), 'off', 'depth'), parts along dimension 0
There are 2 independent parts, one for each index of `parts`. A program takes and returns all parts, laid end to end along the dimension named above; an argument that names none is the same for every part. Nothing has to cross between parts.
Inputs may be any that keep to these rules, and one draw needn't show every extreme that they name: Each value appears once; image column k holds offset offset_of[k] - 32 cells along x.
All inputs are finite; a program needn't handle non-finite values.
Results may differ from a plain program's by a relative error of at most 0.0003.
Values may be sent and summed in bfloat16 or wider, within the bound.
A program may use at most 64 MiB of HBM per device.

v0:
```python
import jax
import jax.numpy as jnp
from jax import lax
from jax.sharding import PartitionSpec as P

H = 64


STENCIL = (-205.0 / 72.0, 8.0 / 5.0, -1.0 / 5.0, 8.0 / 315.0, -1.0 / 560.0)


def extended_2(cells, sides, width):
    for axis, dim in sides:
        count = lax.axis_size(axis)
        ends = count - 1
        head = lax.slice_in_dim(cells, 0, width, axis=dim)
        tail = lax.slice_in_dim(cells, cells.shape[dim] - width, cells.shape[dim], axis=dim)
        cells = jnp.concatenate(
            [
                lax.ppermute(tail, axis, [(i, (i + 1) % count) for i in range(ends)]),
                cells,
                lax.ppermute(head, axis, [((i + 1) % count, i) for i in range(ends)]),
            ],
            axis=dim,
        )
    return cells


def laplace(padded, rows_y, rows_z, cols_x):
    extended = jnp.pad(padded, ((0, 0), (0, 0), (4, 4)))
    centre = extended[4 : 4 + rows_y, 4 : 4 + rows_z, 4 : 4 + cols_x]
    running = 3.0 * STENCIL[0] * centre
    for radius in range(1, 5):
        beside_all = extended[4 + radius : 4 + radius + rows_y, 4 : 4 + rows_z, 4 : 4 + cols_x]
        beside_all = (
            beside_all + extended[4 - radius : 4 - radius + rows_y, 4 : 4 + rows_z, 4 : 4 + cols_x]
        )
        beside_all = (
            beside_all + extended[4 : 4 + rows_y, 4 + radius : 4 + radius + rows_z, 4 : 4 + cols_x]
        )
        beside_all = (
            beside_all + extended[4 : 4 + rows_y, 4 - radius : 4 - radius + rows_z, 4 : 4 + cols_x]
        )
        beside_all = (
            beside_all + extended[4 : 4 + rows_y, 4 : 4 + rows_z, 4 + radius : 4 + radius + cols_x]
        )
        beside_all = (
            beside_all + extended[4 : 4 + rows_y, 4 : 4 + rows_z, 4 - radius : 4 - radius + cols_x]
        )
        running = running + STENCIL[radius] * beside_all
    return running


def on_device(image, offset_of, background, wave_now, wave_prev, courant):
    slab_rows = wave_now.shape[1]
    depth_rows = wave_now.shape[2]
    width_x = wave_now.shape[3]
    local_cols = image.shape[0]
    half_span = H // 2
    gathered = lax.all_gather(background, "off", axis=1, tiled=True)
    extended_bg = jnp.pad(gathered[0], ((0, 0), (0, 0), (half_span, half_span)))
    first_index = jnp.asarray(jnp.int32(0), jnp.int32)

    def add_column(column, running):
        offset_cells = offset_of[column] - half_span
        whole_col = lax.dynamic_index_in_dim(image, column, 0, keepdims=False)
        starts = (first_index, jnp.zeros((), jnp.int32), half_span - offset_cells)
        shifted = lax.dynamic_slice(
            extended_bg, starts, (slab_rows * lax.axis_size("off"), depth_rows, width_x)
        )
        return running + whole_col.astype(jnp.float32) * shifted.astype(jnp.float32)

    own_source = lax.psum_scatter(
        lax.fori_loop(
            0,
            local_cols,
            add_column,
            jnp.zeros((slab_rows * lax.axis_size("off"), depth_rows, width_x), jnp.float32),
        ),
        "off",
        scatter_dimension=0,
        tiled=True,
    )
    padded = extended_2(wave_now[0], (("off", 0), ("depth", 1)), 4)
    bending = laplace(padded, slab_rows, depth_rows, width_x)
    stepped = 2.0 * wave_now[0] - wave_prev[0] + courant * (bending + own_source)
    return stepped[None]


def solution(mesh):
    return jax.shard_map(
        on_device,
        mesh=mesh,
        in_specs=(
            P("off", None, "depth", None),
            P("off"),
            P(("parts", "shot"), "off", "depth", None),
            P(("parts", "shot"), "off", "depth", None),
            P(("parts", "shot"), "off", "depth", None),
            P("off", "depth", None),
        ),
        out_specs=P(("parts", "shot"), "off", "depth", None),
        check_vma=False,
    )
```

profile of v0, /device:TPU:0, one launch (start us, length us, event | category | flops | bytes accessed | tf_op | source)
XLA Modules:
  0.0 105.7 jit_solution(5302099178217128605)
XLA Ops:
  6.5 0.0 reduce-scatter.2.cloned.1.call-start
  6.5 15.9 %all_gather.3 = bf16[1,32,16,256]{3,2,0,1:T(8,128)(2,1)S(1)} all-gather(bf16[1,8,16,256]{3,2,0,1:T(8,128)(2,1)} %bitcast.29), channel_id=1, replica_groups=mesh['parts'=2,'off'=4,'depth'=2,'shot'=2] {'off'}, dimensions={1}, use_global_device_ids=true | all-gather | bytes 327680 | tf_op jit(solution)/shard_map/all_gather | solution.py:60
  22.4 0.2 pad.9
  22.6 0.0 copy-start.1
  22.6 0.0 copy-start.2
  22.6 0.0 copy-start.3
  22.6 50.0 %while.16 = (s32[]{:T(128)}, f32[32,16,256]{2,1,0:T(8,128)S(1)}, bf16[16,32,16,256]{3,2,1,0:T(8,128)(2,1)}, s32[16]{0:T(128)}, bf16[32,16,320]{2,1,0:T(8,128)(2,...) while((s32[]{:T(128)}, f32[32,16,256]{2,1,0:T(8,128)S(1)}, ...), condition=%wide.region_1.2_spmd.clone, body=%wide.region_0.1_spmd.clone.sunk | while | flops 655368 | bytes 1573061 | solution.py:74
  22.7 1.3 %dynamic_slice.41 = s32[1]{0:T(128)} dynamic-slice(s32[16]{0:T(128)} %get-tuple-element.227, s32[]{:T(128)S(6)} %copy.10), dynamic_slice_sizes={1} | dynamic-slice | bytes 12 | tf_op jit(solution)/shard_map/while/body/eval_jaxpr/dynamic_slice | solution.py:65
  24.6 1.2 %fusion.37 = f32[32,16,256]{2,1,0:T(8,128)S(1)} fusion(f32[32,16,256]{2,1,0:T(8,128)S(1)} %get-tuple-element.215, bf16[32,16,320]{2,1,0:T(8,128)(2,1)S(1)} %get-tuple-element.228, s32[]{:T(128)S(6)} %select_n.22, bf16[16,32,16,256]{3,2,1,0:T(8,128)(2,1)} %get-tuple-element.226, s32[]{:T(128)S(6)} %copy.10, pred[]{:T(512)S(6)} %compare.23), kind=kLoop, calls=%fused_computation.1.clone.1 | loop fusion | flops 655360 | bytes 1572873 | tf_op jit(solution)/shard_map/while/body/eval_jaxpr/add | solution.py:71
  25.9 1.3 %dynamic_slice.41 = s32[1]{0:T(128)} dynamic-slice(s32[16]{0:T(128)} %get-tuple-element.227, s32[]{:T(128)S(6)} %copy.10), dynamic_slice_sizes={1} | dynamic-slice | bytes 12 | tf_op jit(solution)/shard_map/while/body/eval_jaxpr/dynamic_slice | solution.py:65
  27.8 1.2 %fusion.37 = f32[32,16,256]{2,1,0:T(8,128)S(1)} fusion(f32[32,16,256]{2,1,0:T(8,128)S(1)} %get-tuple-element.215, bf16[32,16,320]{2,1,0:T(8,128)(2,1)S(1)} %get-tuple-element.228, s32[]{:T(128)S(6)} %select_n.22, bf16[16,32,16,256]{3,2,1,0:T(8,128)(2,1)} %get-tuple-element.226, s32[]{:T(128)S(6)} %copy.10, pred[]{:T(512)S(6)} %compare.23), kind=kLoop, calls=%fused_computation.1.clone.1 | loop fusion | flops 655360 | bytes 1572873 | tf_op jit(solution)/shard_map/while/body/eval_jaxpr/add | solution.py:71
  29.0 1.3 %dynamic_slice.41 = s32[1]{0:T(128)} dynamic-slice(s32[16]{0:T(128)} %get-tuple-element.227, s32[]{:T(128)S(6)} %copy.10), dynamic_slice_sizes={1} | dynamic-slice | bytes 12 | tf_op jit(solution)/shard_map/while/body/eval_jaxpr/dynamic_slice | solution.py:65
  30.9 1.2 %fusion.37 = f32[32,16,256]{2,1,0:T(8,128)S(1)} fusion(f32[32,16,256]{2,1,0:T(8,128)S(1)} %get-tuple-element.215, bf16[32,16,320]{2,1,0:T(8,128)(2,1)S(1)} %get-tuple-element.228, s32[]{:T(128)S(6)} %select_n.22, bf16[16,32,16,256]{3,2,1,0:T(8,128)(2,1)} %get-tuple-element.226, s32[]{:T(128)S(6)} %copy.10, pred[]{:T(512)S(6)} %compare.23), kind=kLoop, calls=%fused_computation.1.clone.1 | loop fusion | flops 655360 | bytes 1572873 | tf_op jit(solution)/shard_map/while/body/eval_jaxpr/add | solution.py:71
  32.1 1.3 %dynamic_slice.41 = s32[1]{0:T(128)} dynamic-slice(s32[16]{0:T(128)} %get-tuple-element.227, s32[]{:T(128)S(6)} %copy.10), dynamic_slice_sizes={1} | dynamic-slice | bytes 12 | tf_op jit(solution)/shard_map/while/body/eval_jaxpr/dynamic_slice | solution.py:65
  34.0 1.2 %fusion.37 = f32[32,16,256]{2,1,0:T(8,128)S(1)} fusion(f32[32,16,256]{2,1,0:T(8,128)S(1)} %get-tuple-element.215, bf16[32,16,320]{2,1,0:T(8,128)(2,1)S(1)} %get-tuple-element.228, s32[]{:T(128)S(6)} %select_n.22, bf16[16,32,16,256]{3,2,1,0:T(8,128)(2,1)} %get-tuple-element.226, s32[]{:T(128)S(6)} %copy.10, pred[]{:T(512)S(6)} %compare.23), kind=kLoop, calls=%fused_computation.1.clone.1 | loop fusion | flops 655360 | bytes 1572873 | tf_op jit(solution)/shard_map/while/body/eval_jaxpr/add | solution.py:71
  35.2 1.3 %dynamic_slice.41 = s32[1]{0:T(128)} dynamic-slice(s32[16]{0:T(128)} %get-tuple-element.227, s32[]{:T(128)S(6)} %copy.10), dynamic_slice_sizes={1} | dynamic-slice | bytes 12 | tf_op jit(solution)/shard_map/while/body/eval_jaxpr/dynamic_slice | solution.py:65
  37.1 1.2 %fusion.37 = f32[32,16,256]{2,1,0:T(8,128)S(1)} fusion(f32[32,16,256]{2,1,0:T(8,128)S(1)} %get-tuple-element.215, bf16[32,16,320]{2,1,0:T(8,128)(2,1)S(1)} %get-tuple-element.228, s32[]{:T(128)S(6)} %select_n.22, bf16[16,32,16,256]{3,2,1,0:T(8,128)(2,1)} %get-tuple-element.226, s32[]{:T(128)S(6)} %copy.10, pred[]{:T(512)S(6)} %compare.23), kind=kLoop, calls=%fused_computation.1.clone.1 | loop fusion | flops 655360 | bytes 1572873 | tf_op jit(solution)/shard_map/while/body/eval_jaxpr/add | solution.py:71
  38.3 1.3 %dynamic_slice.41 = s32[1]{0:T(128)} dynamic-slice(s32[16]{0:T(128)} %get-tuple-element.227, s32[]{:T(128)S(6)} %copy.10), dynamic_slice_sizes={1} | dynamic-slice | bytes 12 | tf_op jit(solution)/shard_map/while/body/eval_jaxpr/dynamic_slice | solution.py:65
  40.2 1.2 %fusion.37 = f32[32,16,256]{2,1,0:T(8,128)S(1)} fusion(f32[32,16,256]{2,1,0:T(8,128)S(1)} %get-tuple-element.215, bf16[32,16,320]{2,1,0:T(8,128)(2,1)S(1)} %get-tuple-element.228, s32[]{:T(128)S(6)} %select_n.22, bf16[16,32,16,256]{3,2,1,0:T(8,128)(2,1)} %get-tuple-element.226, s32[]{:T(128)S(6)} %copy.10, pred[]{:T(512)S(6)} %compare.23), kind=kLoop, calls=%fused_computation.1.clone.1 | loop fusion | flops 655360 | bytes 1572873 | tf_op jit(solution)/shard_map/while/body/eval_jaxpr/add | solution.py:71
  41.4 1.3 %dynamic_slice.41 = s32[1]{0:T(128)} dynamic-slice(s32[16]{0:T(128)} %get-tuple-element.227, s32[]{:T(128)S(6)} %copy.10), dynamic_slice_sizes={1} | dynamic-slice | bytes 12 | tf_op jit(solution)/shard_map/while/body/eval_jaxpr/dynamic_slice | solution.py:65
  43.4 1.2 %fusion.37 = f32[32,16,256]{2,1,0:T(8,128)S(1)} fusion(f32[32,16,256]{2,1,0:T(8,128)S(1)} %get-tuple-element.215, bf16[32,16,320]{2,1,0:T(8,128)(2,1)S(1)} %get-tuple-element.228, s32[]{:T(128)S(6)} %select_n.22, bf16[16,32,16,256]{3,2,1,0:T(8,128)(2,1)} %get-tuple-element.226, s32[]{:T(128)S(6)} %copy.10, pred[]{:T(512)S(6)} %compare.23), kind=kLoop, calls=%fused_computation.1.clone.1 | loop fusion | flops 655360 | bytes 1572873 | tf_op jit(solution)/shard_map/while/body/eval_jaxpr/add | solution.py:71
  44.6 1.3 %dynamic_slice.41 = s32[1]{0:T(128)} dynamic-slice(s32[16]{0:T(128)} %get-tuple-element.227, s32[]{:T(128)S(6)} %copy.10), dynamic_slice_sizes={1} | dynamic-slice | bytes 12 | tf_op jit(solution)/shard_map/while/body/eval_jaxpr/dynamic_slice | solution.py:65
  46.5 1.2 %fusion.37 = f32[32,16,256]{2,1,0:T(8,128)S(1)} fusion(f32[32,16,256]{2,1,0:T(8,128)S(1)} %get-tuple-element.215, bf16[32,16,320]{2,1,0:T(8,128)(2,1)S(1)} %get-tuple-element.228, s32[]{:T(128)S(6)} %select_n.22, bf16[16,32,16,256]{3,2,1,0:T(8,128)(2,1)} %get-tuple-element.226, s32[]{:T(128)S(6)} %copy.10, pred[]{:T(512)S(6)} %compare.23), kind=kLoop, calls=%fused_computation.1.clone.1 | loop fusion | flops 655360 | bytes 1572873 | tf_op jit(solution)/shard_map/while/body/eval_jaxpr/add | solution.py:71
  47.7 1.3 %dynamic_slice.41 = s32[1]{0:T(128)} dynamic-slice(s32[16]{0:T(128)} %get-tuple-element.227, s32[]{:T(128)S(6)} %copy.10), dynamic_slice_sizes={1} | dynamic-slice | bytes 12 | tf_op jit(solution)/shard_map/while/body/eval_jaxpr/dynamic_slice | solution.py:65
  49.6 1.2 %fusion.37 = f32[32,16,256]{2,1,0:T(8,128)S(1)} fusion(f32[32,16,256]{2,1,0:T(8,128)S(1)} %get-tuple-element.215, bf16[32,16,320]{2,1,0:T(8,128)(2,1)S(1)} %get-tuple-element.228, s32[]{:T(128)S(6)} %select_n.22, bf16[16,32,16,256]{3,2,1,0:T(8,128)(2,1)} %get-tuple-element.226, s32[]{:T(128)S(6)} %copy.10, pred[]{:T(512)S(6)} %compare.23), kind=kLoop, calls=%fused_computation.1.clone.1 | loop fusion | flops 655360 | bytes 1572873 | tf_op jit(solution)/shard_map/while/body/eval_jaxpr/add | solution.py:71
  50.8 1.3 %dynamic_slice.41 = s32[1]{0:T(128)} dynamic-slice(s32[16]{0:T(128)} %get-tuple-element.227, s32[]{:T(128)S(6)} %copy.10), dynamic_slice_sizes={1} | dynamic-slice | bytes 12 | tf_op jit(solution)/shard_map/while/body/eval_jaxpr/dynamic_slice | solution.py:65
  52.7 1.2 %fusion.37 = f32[32,16,256]{2,1,0:T(8,128)S(1)} fusion(f32[32,16,256]{2,1,0:T(8,128)S(1)} %get-tuple-element.215, bf16[32,16,320]{2,1,0:T(8,128)(2,1)S(1)} %get-tuple-element.228, s32[]{:T(128)S(6)} %select_n.22, bf16[16,32,16,256]{3,2,1,0:T(8,128)(2,1)} %get-tuple-element.226, s32[]{:T(128)S(6)} %copy.10, pred[]{:T(512)S(6)} %compare.23), kind=kLoop, calls=%fused_computation.1.clone.1 | loop fusion | flops 655360 | bytes 1572873 | tf_op jit(solution)/shard_map/while/body/eval_jaxpr/add | solution.py:71
  53.9 1.3 %dynamic_slice.41 = s32[1]{0:T(128)} dynamic-slice(s32[16]{0:T(128)} %get-tuple-element.227, s32[]{:T(128)S(6)} %copy.10), dynamic_slice_sizes={1} | dynamic-slice | bytes 12 | tf_op jit(solution)/shard_map/while/body/eval_jaxpr/dynamic_slice | solution.py:65
  55.8 1.2 %fusion.37 = f32[32,16,256]{2,1,0:T(8,128)S(1)} fusion(f32[32,16,256]{2,1,0:T(8,128)S(1)} %get-tuple-element.215, bf16[32,16,320]{2,1,0:T(8,128)(2,1)S(1)} %get-tuple-element.228, s32[]{:T(128)S(6)} %select_n.22, bf16[16,32,16,256]{3,2,1,0:T(8,128)(2,1)} %get-tuple-element.226, s32[]{:T(128)S(6)} %copy.10, pred[]{:T(512)S(6)} %compare.23), kind=kLoop, calls=%fused_computation.1.clone.1 | loop fusion | flops 655360 | bytes 1572873 | tf_op jit(solution)/shard_map/while/body/eval_jaxpr/add | solution.py:71
  57.0 1.3 %dynamic_slice.41 = s32[1]{0:T(128)} dynamic-slice(s32[16]{0:T(128)} %get-tuple-element.227, s32[]{:T(128)S(6)} %copy.10), dynamic_slice_sizes={1} | dynamic-slice | bytes 12 | tf_op jit(solution)/shard_map/while/body/eval_jaxpr/dynamic_slice | solution.py:65
  58.9 1.2 %fusion.37 = f32[32,16,256]{2,1,0:T(8,128)S(1)} fusion(f32[32,16,256]{2,1,0:T(8,128)S(1)} %get-tuple-element.215, bf16[32,16,320]{2,1,0:T(8,128)(2,1)S(1)} %get-tuple-element.228, s32[]{:T(128)S(6)} %select_n.22, bf16[16,32,16,256]{3,2,1,0:T(8,128)(2,1)} %get-tuple-element.226, s32[]{:T(128)S(6)} %copy.10, pred[]{:T(512)S(6)} %compare.23), kind=kLoop, calls=%fused_computation.1.clone.1 | loop fusion | flops 655360 | bytes 1572873 | tf_op jit(solution)/shard_map/while/body/eval_jaxpr/add | solution.py:71
  60.2 1.3 %dynamic_slice.41 = s32[1]{0:T(128)} dynamic-slice(s32[16]{0:T(128)} %get-tuple-element.227, s32[]{:T(128)S(6)} %copy.10), dynamic_slice_sizes={1} | dynamic-slice | bytes 12 | tf_op jit(solution)/shard_map/while/body/eval_jaxpr/dynamic_slice | solution.py:65
  62.1 1.2 %fusion.37 = f32[32,16,256]{2,1,0:T(8,128)S(1)} fusion(f32[32,16,256]{2,1,0:T(8,128)S(1)} %get-tuple-element.215, bf16[32,16,320]{2,1,0:T(8,128)(2,1)S(1)} %get-tuple-element.228, s32[]{:T(128)S(6)} %select_n.22, bf16[16,32,16,256]{3,2,1,0:T(8,128)(2,1)} %get-tuple-element.226, s32[]{:T(128)S(6)} %copy.10, pred[]{:T(512)S(6)} %compare.23), kind=kLoop, calls=%fused_computation.1.clone.1 | loop fusion | flops 655360 | bytes 1572873 | tf_op jit(solution)/shard_map/while/body/eval_jaxpr/add | solution.py:71
  63.3 1.3 %dynamic_slice.41 = s32[1]{0:T(128)} dynamic-slice(s32[16]{0:T(128)} %get-tuple-element.227, s32[]{:T(128)S(6)} %copy.10), dynamic_slice_sizes={1} | dynamic-slice | bytes 12 | tf_op jit(solution)/shard_map/while/body/eval_jaxpr/dynamic_slice | solution.py:65
  65.2 1.2 %fusion.37 = f32[32,16,256]{2,1,0:T(8,128)S(1)} fusion(f32[32,16,256]{2,1,0:T(8,128)S(1)} %get-tuple-element.215, bf16[32,16,320]{2,1,0:T(8,128)(2,1)S(1)} %get-tuple-element.228, s32[]{:T(128)S(6)} %select_n.22, bf16[16,32,16,256]{3,2,1,0:T(8,128)(2,1)} %get-tuple-element.226, s32[]{:T(128)S(6)} %copy.10, pred[]{:T(512)S(6)} %compare.23), kind=kLoop, calls=%fused_computation.1.clone.1 | loop fusion | flops 655360 | bytes 1572873 | tf_op jit(solution)/shard_map/while/body/eval_jaxpr/add | solution.py:71
  66.4 1.3 %dynamic_slice.41 = s32[1]{0:T(128)} dynamic-slice(s32[16]{0:T(128)} %get-tuple-element.227, s32[]{:T(128)S(6)} %copy.10), dynamic_slice_sizes={1} | dynamic-slice | bytes 12 | tf_op jit(solution)/shard_map/while/body/eval_jaxpr/dynamic_slice | solution.py:65
  68.3 1.2 %fusion.37 = f32[32,16,256]{2,1,0:T(8,128)S(1)} fusion(f32[32,16,256]{2,1,0:T(8,128)S(1)} %get-tuple-element.215, bf16[32,16,320]{2,1,0:T(8,128)(2,1)S(1)} %get-tuple-element.228, s32[]{:T(128)S(6)} %select_n.22, bf16[16,32,16,256]{3,2,1,0:T(8,128)(2,1)} %get-tuple-element.226, s32[]{:T(128)S(6)} %copy.10, pred[]{:T(512)S(6)} %compare.23), kind=kLoop, calls=%fused_computation.1.clone.1 | loop fusion | flops 655360 | bytes 1572873 | tf_op jit(solution)/shard_map/while/body/eval_jaxpr/add | solution.py:71
  69.5 1.3 %dynamic_slice.41 = s32[1]{0:T(128)} dynamic-slice(s32[16]{0:T(128)} %get-tuple-element.227, s32[]{:T(128)S(6)} %copy.10), dynamic_slice_sizes={1} | dynamic-slice | bytes 12 | tf_op jit(solution)/shard_map/while/body/eval_jaxpr/dynamic_slice | solution.py:65
  71.4 1.2 %fusion.37 = f32[32,16,256]{2,1,0:T(8,128)S(1)} fusion(f32[32,16,256]{2,1,0:T(8,128)S(1)} %get-tuple-element.215, bf16[32,16,320]{2,1,0:T(8,128)(2,1)S(1)} %get-tuple-element.228, s32[]{:T(128)S(6)} %select_n.22, bf16[16,32,16,256]{3,2,1,0:T(8,128)(2,1)} %get-tuple-element.226, s32[]{:T(128)S(6)} %copy.10, pred[]{:T(512)S(6)} %compare.23), kind=kLoop, calls=%fused_computation.1.clone.1 | loop fusion | flops 655360 | bytes 1572873 | tf_op jit(solution)/shard_map/while/body/eval_jaxpr/add | solution.py:71
  72.6 0.0 copy-start
  72.6 0.8 copy-done
  73.4 0.0 reduce-scatter.2.cloned.1.call-update
  73.5 0.0 copy-done.1
  73.5 1.3 %collective-permute-start = (f32[4,16,256]{2,1,0:T(8,128)S(1)}, f32[4,16,256]{2,1,0:T(8,128)S(1)}, u32[]{:S(2)}, u32[]{:S(2)}) collective-permute-start(f32[4,16,256]{2,1,0:T(8,128)S(1)} %get-tuple-element.171), channel_id=1, source_target_pairs={{4,0},{8,4},{12,8},{5,1},{9,5},{13,9},{6,2},{10,6},{14,10},{7,3},{... | collective-permute-start | bytes 196616 | tf_op jit(solution)/shard_map/ppermute | solution.py:22
  74.8 4.5 %collective-permute-start.1 = (f32[4,16,256]{2,1,0:T(8,128)S(1)}, f32[4,16,256]{2,1,0:T(8,128)S(1)}, u32[]{:S(2)}, u32[]{:S(2)}) collective-permute-start(f32[4,16,256]{2,1,0:T(8,128)S(1)} %get-tuple-element.172), channel_id=1, source_target_pairs={{0,4},{4,8},{8,12},{1,5},{5,9},{9,13},{2,6},{6,10},{10,14},{3,7},{... | collective-permute-start | bytes 196616 | tf_op jit(solution)/shard_map/ppermute | solution.py:20
  79.3 0.3 collective-permute-done
  79.6 1.6 %collective-permute-done.1 = f32[4,16,256]{2,1,0:T(8,128)S(1)} collective-permute-done((f32[4,16,256]{2,1,0:T(8,128)S(1)}, f32[4,16,256]{2,1,0:T(8,128)S(1)}, u32[]{:S(2)}, u32[]{:S(2)}) %collective-permute-start.1) | collective-permute-done | bytes 65568 | tf_op jit(solution)/shard_map/ppermute | solution.py:20
  81.3 3.4 %collective-permute-start.3 = (f32[16,4,256]{2,1,0:T(4,128)S(1)}, f32[16,4,256]{2,1,0:T(4,128)S(1)}, u32[]{:S(2)}, u32[]{:S(2)}) collective-permute-start(f32[16,4,256]{2,1,0:T(4,128)S(1)} %get-tuple-element.169), channel_id=1, source_target_pairs={{0,2},{1,3},{4,6},{5,7},{8,10},{9,11},{12,14},{13,15},{16,18},{17,... | collective-permute-start | bytes 196616 | tf_op jit(solution)/shard_map/ppermute | solution.py:20
  84.7 1.3 %collective-permute-start.2 = (f32[16,4,256]{2,1,0:T(4,128)S(1)}, f32[16,4,256]{2,1,0:T(4,128)S(1)}, u32[]{:S(2)}, u32[]{:S(2)}) collective-permute-start(f32[16,4,256]{2,1,0:T(4,128)S(1)} %get-tuple-element.170), channel_id=1, source_target_pairs={{2,0},{3,1},{6,4},{7,5},{10,8},{11,9},{14,12},{15,13},{18,16},{19,... | collective-permute-start | bytes 196616 | tf_op jit(solution)/shard_map/ppermute | solution.py:22
  86.0 0.6 collective-permute-done.3
  86.5 4.3 %collective-permute-done.2 = f32[16,4,256]{2,1,0:T(4,128)S(1)} collective-permute-done((f32[16,4,256]{2,1,0:T(4,128)S(1)}, f32[16,4,256]{2,1,0:T(4,128)S(1)}, u32[]{:S(2)}, u32[]{:S(2)}) %collective-permute-start.2) | collective-permute-done | bytes 65568 | tf_op jit(solution)/shard_map/ppermute | solution.py:22
  90.8 0.3 select_maximum_fusion
  91.2 0.1 pad_maximum_fusion
  91.2 5.8 %reduce-scatter.2.cloned.1.call-done = f32[8,16,256]{2,1,0:T(8,128)} async-done(((f32[32,16,256]{2,1,0:T(8,128)}), f32[8,16,256]{2,1,0:T(8,128)}) %reduce-scatter.2.cloned.1.call-update) | async-done | bytes 131088 | tf_op jit(solution)/shard_map/reduce_scatter | solution.py:73
  97.0 0.0 copy-done.2
  97.0 0.0 copy-done.3
  97.0 1.9 %fusion.14 = f32[1,8,16,256]{3,2,1,0:T(8,128)} fusion(f32[8,16,256]{2,1,0:T(8,128)S(1)} %copy-done.2, f32[8,16,256]{2,1,0:T(8,128)} %reduce-scatter.2.cloned.1.call-done, f32[8,16,256]{2,1,0:T(8,128)S(1)} %bitcast.27, f32[4,16,256]{2,1,0:T(8,128)S(1)} %collective-permute-done.1, f32[4,16,256]{2,1,0:T(8,128)S(1)} %collective-permute-done, ...), kind=kLoop, calls=%fused_computation.35 | loop fusion | flops 1376256 | bytes 2883584 | tf_op jit(solution)/shard_map/broadcast_in_dim | solution.py:87
  (3 shorter events, 0.0 us)
Async XLA Ops:
  6.5 90.5 %reduce-scatter.2.cloned.1.call-start = ((), (), s32[]{:S(2)}) async-start(), calls=%async_computation.1 | async-start | bytes 655360 | tf_op jit(solution)/shard_map/reduce_scatter | solution.py:73
  22.6 50.8 %copy-start.1 = (f32[1,8,16,256]{3,2,1,0:T(8,128)S(1)}, f32[1,8,16,256]{3,2,1,0:T(8,128)}, u32[]{:S(2)}) copy-start(f32[1,8,16,256]{3,2,1,0:T(8,128)} %param.11) | copy-start | bytes 393220
  22.6 74.4 %copy-start.2 = (f32[8,16,256]{2,1,0:T(8,128)S(1)}, f32[8,16,256]{2,1,0:T(8,128)}, u32[]{:S(2)}) copy-start(f32[8,16,256]{2,1,0:T(8,128)} %param.13) | copy-start | bytes 393220
  22.6 74.4 %copy-start.3 = (f32[1,8,16,256]{3,2,1,0:T(8,128)S(1)}, f32[1,8,16,256]{3,2,1,0:T(8,128)}, u32[]{:S(2)}) copy-start(f32[1,8,16,256]{3,2,1,0:T(8,128)} %param.12) | copy-start | bytes 393220
  72.6 0.8 copy-start
  73.5 6.2 %collective-permute-start = (f32[4,16,256]{2,1,0:T(8,128)S(1)}, f32[4,16,256]{2,1,0:T(8,128)S(1)}, u32[]{:S(2)}, u32[]{:S(2)}) collective-permute-start(f32[4,16,256]{2,1,0:T(8,128)S(1)} %get-tuple-element.171), channel_id=1, source_target_pairs={{4,0},{8,4},{12,8},{5,1},{9,5},{13,9},{6,2},{10,6},{14,10},{7,3},{... | collective-permute-start | bytes 196616 | tf_op jit(solution)/shard_map/ppermute | solution.py:22
  74.8 6.5 %collective-permute-start.1 = (f32[4,16,256]{2,1,0:T(8,128)S(1)}, f32[4,16,256]{2,1,0:T(8,128)S(1)}, u32[]{:S(2)}, u32[]{:S(2)}) collective-permute-start(f32[4,16,256]{2,1,0:T(8,128)S(1)} %get-tuple-element.172), channel_id=1, source_target_pairs={{0,4},{4,8},{8,12},{1,5},{5,9},{9,13},{2,6},{6,10},{10,14},{3,7},{... | collective-permute-start | bytes 196616 | tf_op jit(solution)/shard_map/ppermute | solution.py:20
  81.3 5.3 %collective-permute-start.3 = (f32[16,4,256]{2,1,0:T(4,128)S(1)}, f32[16,4,256]{2,1,0:T(4,128)S(1)}, u32[]{:S(2)}, u32[]{:S(2)}) collective-permute-start(f32[16,4,256]{2,1,0:T(4,128)S(1)} %get-tuple-element.169), channel_id=1, source_target_pairs={{0,2},{1,3},{4,6},{5,7},{8,10},{9,11},{12,14},{13,15},{16,18},{17,... | collective-permute-start | bytes 196616 | tf_op jit(solution)/shard_map/ppermute | solution.py:20
  84.7 6.2 %collective-permute-start.2 = (f32[16,4,256]{2,1,0:T(4,128)S(1)}, f32[16,4,256]{2,1,0:T(4,128)S(1)}, u32[]{:S(2)}, u32[]{:S(2)}) collective-permute-start(f32[16,4,256]{2,1,0:T(4,128)S(1)} %get-tuple-element.170), channel_id=1, source_target_pairs={{2,0},{3,1},{6,4},{7,5},{10,8},{11,9},{14,12},{15,13},{18,16},{19,... | collective-permute-start | bytes 196616 | tf_op jit(solution)/shard_map/ppermute | solution.py:22
Sparse Core Ops, SparseCore 0:
  73.6 23.3 reduce-scatter.1
where the time goes:
time: 107 us; the launch traced here: 106 us
  other arithmetic  21.3 us (20%)
  local copies, waits for them, and re-layouts  21.3 us (20%)
  blocking collectives  15.9 us (15%)
  between operations  13.5 us (13%)
  waiting for transfers between devices  12.6 us (12%)
  loops' own time  10.6 us (10%)
  starting transfers between devices  10.5 us (10%)
    dynamic_slice x16, local copies, waits for them, and re-layouts, add_column(): offset_cells = offset_of[column] - half_span  20.3 us
    add x16, other arithmetic, add_column(): return running + whole_col.astype(jnp.float32) * shifted.astype(jnp.float32)  19 us
    all_gather x1, blocking collectives, on_device(): gathered = lax.all_gather(background, 'off', axis=1, tiled=True)  15.9 us
    another operation x1, loops' own time, on_device(): lax.fori_loop(0, local_cols, add_column, jnp.zeros((slab_rows * lax.axis_...  10.6 us
    ppermute x2, starting transfers between devices, extended_2(): lax.ppermute(tail, axis, [(i, (i + 1) % count) for i in range(ends)])  7.91 us
    reduce_scatter x1, waiting for transfers between devices, on_device(): lax.psum_scatter(lax.fori_loop(0, local_cols, add_column, jnp.zeros((slab...  5.78 us
    ppermute x2, waiting for transfers between devices, extended_2(): lax.ppermute(head, axis, [((i + 1) % count, i) for i in range(ends)])  4.58 us
    ppermute x2, starting transfers between devices, extended_2(): lax.ppermute(head, axis, [((i + 1) % count, i) for i in range(ends)])  2.58 us
  transfers between devices with their start and end apart: 5, of which 5 were waited for; matrix products, arithmetic and copies ran while one was open for 0% of the time, Pallas kernels for 0%

commit v1 on v0

v1 whole, which is shorter than its diff:
```python
import functools

import jax
import jax.numpy as jnp
from jax import lax
from jax.experimental import pallas as pl
from jax.experimental.pallas import tpu as pltpu
from jax.sharding import PartitionSpec as P

H = 64
STENCIL = (-205.0 / 72.0, 8.0 / 5.0, -1.0 / 5.0, 8.0 / 315.0, -1.0 / 560.0)
R = 4
MESH = pl.DeviceIdType.MESH


def kernel(
    n, nd,
    off_ref, img_hbm, bg_hbm, now_hbm, prev_hbm, cour_hbm,
    out_ref,
    img, bg, wext, prev, cour, shift, acc, fin, part_out, part_in,
    load_sem, img_sem, bg_send, bg_recv, halo_send, halo_recv, p_send, p_recv,
):
    K, _, Z, X = img.shape
    Y = out_ref.shape[1]
    me = lax.axis_index("off")
    dep = lax.axis_index("depth")
    has = {"l": me > 0, "r": me < n - 1, "u": dep > 0, "d": dep < nd - 1}
    near = {"l": {"off": me - 1}, "r": {"off": me + 1},
            "u": {"depth": dep - 1}, "d": {"depth": dep + 1}}

    own = wext.at[pl.ds(R, Y), pl.ds(8, Z), :]
    ld_bg = pltpu.make_async_copy(bg_hbm.at[0], bg.at[me], load_sem.at[0])
    ld_now = pltpu.make_async_copy(now_hbm.at[0], own, load_sem.at[1])
    ld_prev = pltpu.make_async_copy(prev_hbm.at[0], prev, load_sem.at[2])
    ld_cour = pltpu.make_async_copy(cour_hbm, cour, load_sem.at[3])
    ld_bg.start()
    ld_now.start()

    def img_load(j):
        rows = pl.ds(j * Y, Y)
        return pltpu.make_async_copy(img_hbm.at[:, rows], img.at[:, rows], img_sem.at[j])

    img_load(me).start()
    for t in range(1, n):
        @pl.when(me - t >= 0)
        def _():
            img_load(me - t).start()

        @pl.when(me + t < n)
        def _():
            img_load(me + t).start()
    ld_prev.start()
    ld_cour.start()

    barrier = pltpu.get_barrier_semaphore()
    for side in "lrud":
        @pl.when(has[side])
        def _():
            pl.semaphore_signal(barrier, inc=1, device_id=near[side], device_id_type=MESH)

    def clear(rows, cols):
        wext[rows, cols, :] = jnp.zeros((rows.size, cols.size, X), jnp.float32)

    edge = {"l": (pl.ds(0, R), pl.ds(8, Z)), "r": (pl.ds(R + Y, R), pl.ds(8, Z)),
            "u": (pl.ds(R, Y), pl.ds(0, 8)), "d": (pl.ds(R, Y), pl.ds(8 + Z, 8))}
    for side in "lrud":
        @pl.when(jnp.logical_not(has[side]))
        def _():
            clear(*edge[side])

    lead = lax.broadcasted_iota(jnp.int32, (X, X), 1) - lax.broadcasted_iota(jnp.int32, (X, X), 0)

    def build(k, carry):
        h = off_ref[k] - H // 2
        shift[k] = jnp.where(lead == h, 1.0, 0.0).astype(jnp.bfloat16)
        return carry

    half = K // 2
    lax.fori_loop(0, half, build, 0)
    ld_bg.wait()
    ld_now.wait()
    count = sum(has[s].astype(jnp.int32) for s in "lrud")
    pl.semaphore_wait(barrier, count)

    def bg_copy(j, side, slot):
        return pltpu.make_async_remote_copy(
            src_ref=bg.at[j], dst_ref=bg.at[j], send_sem=bg_send.at[slot, j],
            recv_sem=bg_recv.at[j], device_id=near[side], device_id_type=MESH)

    mine = {"l": (pl.ds(R, R), pl.ds(8, Z)), "r": (pl.ds(Y, R), pl.ds(8, Z)),
            "u": (pl.ds(R, Y), pl.ds(8, 8)), "d": (pl.ds(R, Y), pl.ds(Z, 8))}
    other = {"l": "r", "r": "l", "u": "d", "d": "u"}
    num = {"l": 0, "r": 1, "u": 2, "d": 3}

    def halo_copy(side):
        there = other[side]
        return pltpu.make_async_remote_copy(
            src_ref=wext.at[mine[side][0], mine[side][1], :],
            dst_ref=wext.at[edge[there][0], edge[there][1], :],
            send_sem=halo_send.at[num[side]], recv_sem=halo_recv.at[num[there]],
            device_id=near[side], device_id_type=MESH)

    for slot, side in enumerate("lr"):
        @pl.when(has[side])
        def _():
            bg_copy(me, side, slot).start()
    for side in "udlr":
        @pl.when(has[side])
        def _():
            halo_copy(side).start()

    lax.fori_loop(half, K, build, 0)

    group = 4 if K % 4 == 0 else 1

    def partial(j, dst, slot):
        lhs = bg[j].reshape(Y * Z, X)
        rows = pl.ds(j * Y, Y)

        def body(g, carry):
            total = None
            for m in range(group):
                k = g * group + m
                moved = jnp.dot(lhs, shift[k], preferred_element_type=jnp.float32)
                term = img[k, rows].astype(jnp.float32) * moved.reshape(Y, Z, X)
                total = term if total is None else total + term

            @pl.when(g == 0)
            def _():
                dst[slot] = total

            @pl.when(g > 0)
            def _():
                dst[slot] = dst[slot] + total
            return carry

        lax.fori_loop(0, K // group, body, 0)

    def part_copy(j):
        return pltpu.make_async_remote_copy(
            src_ref=part_out.at[j], dst_ref=part_in.at[me], send_sem=p_send.at[j],
            recv_sem=p_recv.at[me], device_id={"off": j}, device_id_type=MESH)

    def part_arrival(j):
        return pltpu.make_async_remote_copy(
            src_ref=part_out.at[j], dst_ref=part_in.at[j], send_sem=p_send.at[j],
            recv_sem=p_recv.at[j], device_id={"off": j}, device_id_type=MESH)

    img_load(me).wait()
    partial(me, acc, 0)

    for t in range(1, n):
        for j, ok, onward, slot, side in (
            (me - t, me - t >= 0, me < n - 1, 1, "r"),
            (me + t, me + t < n, me > 0, 0, "l"),
        ):
            @pl.when(ok)
            def _():
                bg_copy(j, side, slot).wait_recv()

                @pl.when(onward)
                def _():
                    bg_copy(j, side, slot).start()
        for j, ok in ((me - t, me - t >= 0), (me + t, me + t < n)):
            @pl.when(ok)
            def _():
                img_load(j).wait()
                partial(j, part_out, j)
                part_copy(j).start()

    ld_prev.wait()
    ld_cour.wait()
    for side in "lrud":
        @pl.when(has[side])
        def _():
            halo_copy(side).wait_send()
            pltpu.make_async_remote_copy(
                src_ref=wext.at[mine[side][0], mine[side][1], :],
                dst_ref=wext.at[edge[side][0], edge[side][1], :],
                send_sem=halo_send.at[num[side]], recv_sem=halo_recv.at[num[side]],
                device_id=near[side], device_id_type=MESH).wait_recv()

    lane = lax.broadcasted_iota(jnp.int32, (Z, X), 1)

    def plane(y, carry):
        centre = wext[y + R, pl.ds(8, Z), :]
        running = 3.0 * STENCIL[0] * centre
        for r in range(1, R + 1):
            beside = wext[y + R + r, pl.ds(8, Z), :] + wext[y + R - r, pl.ds(8, Z), :]
            beside = beside + wext[y + R, pl.ds(8 + r, Z), :]
            beside = beside + wext[y + R, pl.ds(8 - r, Z), :]
            beside = beside + jnp.where(lane < X - r, pltpu.roll(centre, X - r, 1), 0.0)
            beside = beside + jnp.where(lane >= r, pltpu.roll(centre, r, 1), 0.0)
            running = running + STENCIL[r] * beside
        fin[y] = 2.0 * centre - prev[y] + cour[y] * (running + acc[0, y])
        return carry

    lax.fori_loop(0, Y, plane, 0)

    for t in range(1, n):
        for j, ok in ((me - t, me - t >= 0), (me + t, me + t < n)):
            @pl.when(ok)
            def _():
                part_arrival(j).wait_recv()
                fin[...] = fin[...] + cour[...] * part_in[j]
    out_ref[0] = fin[...]

    for slot, side in enumerate("lr"):
        @pl.when(has[side])
        def _():
            bg_copy(me, side, slot).wait_send()
    for t in range(1, n):
        for j, ok, onward, slot, side in (
            (me - t, me - t >= 0, me < n - 1, 1, "r"),
            (me + t, me + t < n, me > 0, 0, "l"),
        ):
            @pl.when(ok)
            def _():
                part_copy(j).wait_send()

                @pl.when(onward)
                def _():
                    bg_copy(j, side, slot).wait_send()


def on_device(n, nd, image, offset_of, background, wave_now, wave_prev, courant):
    K, rows, Z, X = image.shape
    Y = wave_now.shape[1]
    f32 = jnp.float32
    anywhere = pl.BlockSpec(memory_space=pl.ANY)
    dma = pltpu.SemaphoreType.DMA
    return pl.pallas_call(
        functools.partial(kernel, n, nd),
        out_shape=jax.ShapeDtypeStruct(wave_now.shape, f32),
        in_specs=[pl.BlockSpec(memory_space=pltpu.SMEM)] + [anywhere] * 5,
        out_specs=pl.BlockSpec(memory_space=pltpu.VMEM),
        scratch_shapes=[
            pltpu.VMEM((K, rows, Z, X), jnp.bfloat16),
            pltpu.VMEM((n, Y, Z, X), jnp.bfloat16),
            pltpu.VMEM((Y + 2 * R, Z + 16, X), f32),
            pltpu.VMEM((Y, Z, X), f32),
            pltpu.VMEM((Y, Z, X), f32),
            pltpu.VMEM((K, X, X), jnp.bfloat16),
            pltpu.VMEM((1, Y, Z, X), f32),
            pltpu.VMEM((Y, Z, X), f32),
            pltpu.VMEM((n, Y, Z, X), f32),
            pltpu.VMEM((n, Y, Z, X), f32),
            dma((4,)), dma((n,)), dma((2, n)), dma((n,)), dma((4,)), dma((4,)),
            dma((n,)), dma((n,)),
        ],
        compiler_params=pltpu.CompilerParams(
            collective_id=0, has_side_effects=True, vmem_limit_bytes=48 * 2**20),
        name="born_step",
    )(offset_of, image, background, wave_now, wave_prev, courant)


def solution(mesh):
    wave = P(("parts", "shot"), "off", "depth", None)
    return jax.shard_map(
        functools.partial(on_device, mesh.shape["off"], mesh.shape["depth"]),
        mesh=mesh,
        in_specs=(
            P("off", None, "depth", None),
            P("off"),
            wave,
            wave,
            wave,
            P("off", "depth", None),
        ),
        out_specs=wave,
        check_vma=False,
    )
```

time: 107 us -> 31.2 us (0.29)
  Pallas kernels: 0 us -> 23.9 us
  other arithmetic: 21.3 us -> 0 us
  blocking collectives: 15.9 us -> 0 us
  local copies, waits for them, and re-layouts: 21.3 us -> 7.05 us
  between operations: 13.5 us -> 0.02 us
  waiting for transfers between devices: 12.6 us -> 0 us
  loops' own time: 10.6 us -> 0 us
  starting transfers between devices: 10.5 us -> 0 us
    pallas_call x0 -> x1, Pallas kernels: none -> 23.9 us  [on_device(): pl.pallas_call(functools.partial(kernel, n, nd), out_shape=jax.ShapeDtype...]
    dynamic_slice x16 -> x0, local copies, waits for them, and re-layouts: 20.3 us -> none  [add_column(): offset_cells = offset_of[column] - half_span]
    add x16 -> x0, other arithmetic: 19 us -> none  [add_column(): return running + whole_col.astype(jnp.float32) * shifted.astype(jnp.float32)]
    all_gather x1 -> x0, blocking collectives: 15.9 us -> none  [on_device(): gathered = lax.all_gather(background, 'off', axis=1, tiled=True)]
    another operation x1 -> x0, loops' own time: 10.6 us -> none  [on_device(): lax.fori_loop(0, local_cols, add_column, jnp.zeros((slab_rows * lax.axis_...]
    ppermute x4 -> x0, starting transfers between devices: 10.5 us -> none  [the longest x2 7.91 us: extended_2(): lax.ppermute(tail, axis, [(i, (i + 1) % count) for i in range(ends)])]
    ppermute x4 -> x0, waiting for transfers between devices: 6.78 us -> none  [the longest x2 4.58 us: extended_2(): lax.ppermute(head, axis, [((i + 1) % count, i) for i in range(ends)])]
    unnamed x8 -> x13, local copies, waits for them, and re-layouts: 0.82 us -> 7.05 us
  transfers between devices with their start and end apart: 5 -> 0, of which waited for: 5 -> 0; matrix products, arithmetic and copies ran while one was open for 0% -> 0% of each run, Pallas kernels for 0% -> 0%
where the time goes in v1:
time: 31.2 us; the launch traced here: 31 us
  Pallas kernels  23.9 us (77%)
  local copies, waits for them, and re-layouts  7.05 us (23%)
    pallas_call x1, Pallas kernels, on_device(): pl.pallas_call(functools.partial(kernel, n, nd), out_shape=jax.ShapeDtype...  23.9 us
    unnamed x13, local copies, waits for them, and re-layouts  7.05 us

profile of v1, /device:TPU:0, one launch (start us, length us, event | category | flops | bytes accessed | tf_op | source)
XLA Modules:
  0.0 31.0 jit_solution(5784946882014319265)
XLA Ops:
  0.0 0.0 copy-start
  0.0 2.2 %copy-done = bf16[16,32,16,256]{3,2,1,0:T(8,128)(2,1)S(1)} copy-done((bf16[16,32,16,256]{3,2,1,0:T(8,128)(2,1)S(1)}, bf16[16,32,16,256]{3,2,1,0:T(8,128)(2,1)}, u32[]{:S(2)}) %copy-start) | copy-done | bytes 4194328
  2.2 0.0 copy-start.1
  2.2 0.9 %copy-done.1 = f32[1,8,16,256]{3,2,1,0:T(8,128)S(1)} copy-done((f32[1,8,16,256]{3,2,1,0:T(8,128)S(1)}, f32[1,8,16,256]{3,2,1,0:T(8,128)}, u32[]{:S(2)}) %copy-start.1) | copy-done | bytes 131096
  3.1 0.0 copy-start.2
  3.1 0.9 %copy-done.2 = f32[1,8,16,256]{3,2,1,0:T(8,128)S(1)} copy-done((f32[1,8,16,256]{3,2,1,0:T(8,128)S(1)}, f32[1,8,16,256]{3,2,1,0:T(8,128)}, u32[]{:S(2)}) %copy-start.2) | copy-done | bytes 131096
  4.0 0.0 copy-start.3
  4.0 0.9 %copy-done.3 = f32[8,16,256]{2,1,0:T(8,128)S(1)} copy-done((f32[8,16,256]{2,1,0:T(8,128)S(1)}, f32[8,16,256]{2,1,0:T(8,128)}, u32[]{:S(2)}) %copy-start.3) | copy-done | bytes 131096
  4.9 0.0 copy-start.4
  4.9 0.8 %copy-done.4 = bf16[1,8,16,256]{3,2,1,0:T(8,128)(2,1)S(1)} copy-done((bf16[1,8,16,256]{3,2,1,0:T(8,128)(2,1)S(1)}, bf16[1,8,16,256]{3,2,1,0:T(8,128)(2,1)}, u32[]{:S(2)}) %copy-start.4) | copy-done | bytes 65560
  5.7 0.0 copy-start.5
  5.7 0.7 %copy-done.5 = s32[16]{0:T(128)S(1)} copy-done((s32[16]{0:T(128)S(1)}, s32[16]{0:T(128)}, u32[]{:S(2)}) %copy-start.5) | copy-done | bytes 88
  6.4 23.9 %born_step.1 = f32[1,8,16,256]{3,2,1,0:T(8,128)S(1)} custom-call(s32[16]{0:T(128)S(1)} %copy-done.5, bf16[16,32,16,256]{3,2,1,0:T(8,128)(2,1)S(1)} %copy-done, bf16[1,8,16,256]{3,2,1,0:T(8,128)(2,1)S(1)} %copy-done.4, f32[1,8,16,256]{3,2,1,0:T(8,128)S(1)} %copy-done.1, f32[1,8,16,256]{3,2,1,0:T(8,128)S(1)} %copy-done.2, f32[8,16,256]{2,1,0:T(8,128)S(1)} %copy-done.3), custom_call_target="tpu_custom_call" | custom-call | tf_op jit(solution)/shard_map/born_step/pallas_call | solution.py:232
  30.3 0.7 %copy.8 = f32[1,8,16,256]{3,2,1,0:T(8,128)} copy(f32[1,8,16,256]{3,2,1,0:T(8,128)S(1)} %born_step.1) | data formatting | bytes 262144
Async XLA Ops:
  0.0 2.2 %copy-start = (bf16[16,32,16,256]{3,2,1,0:T(8,128)(2,1)S(1)}, bf16[16,32,16,256]{3,2,1,0:T(8,128)(2,1)}, u32[]{:S(2)}) copy-start(bf16[16,32,16,256]{3,2,1,0:T(8,128)(2,1)} %img_hbm.1) | copy-start | bytes 12582916
  2.2 0.9 %copy-start.1 = (f32[1,8,16,256]{3,2,1,0:T(8,128)S(1)}, f32[1,8,16,256]{3,2,1,0:T(8,128)}, u32[]{:S(2)}) copy-start(f32[1,8,16,256]{3,2,1,0:T(8,128)} %now_hbm.1) | copy-start | bytes 393220
  3.1 0.9 %copy-start.2 = (f32[1,8,16,256]{3,2,1,0:T(8,128)S(1)}, f32[1,8,16,256]{3,2,1,0:T(8,128)}, u32[]{:S(2)}) copy-start(f32[1,8,16,256]{3,2,1,0:T(8,128)} %prev_hbm.1) | copy-start | bytes 393220
  4.0 0.9 %copy-start.3 = (f32[8,16,256]{2,1,0:T(8,128)S(1)}, f32[8,16,256]{2,1,0:T(8,128)}, u32[]{:S(2)}) copy-start(f32[8,16,256]{2,1,0:T(8,128)} %cour_hbm.1) | copy-start | bytes 393220
  4.9 0.8 %copy-start.4 = (bf16[1,8,16,256]{3,2,1,0:T(8,128)(2,1)S(1)}, bf16[1,8,16,256]{3,2,1,0:T(8,128)(2,1)}, u32[]{:S(2)}) copy-start(bf16[1,8,16,256]{3,2,1,0:T(8,128)(2,1)} %bg_hbm.1) | copy-start | bytes 196612
  5.7 0.7 %copy-start.5 = (s32[16]{0:T(128)S(1)}, s32[16]{0:T(128)}, u32[]{:S(2)}) copy-start(s32[16]{0:T(128)} %off_ref.1) | copy-start | bytes 196

commit v2 on v1

--- a/solution.py
+++ b/solution.py
@@ -10,6 +10,8 @@
 H = 64
 STENCIL = (-205.0 / 72.0, 8.0 / 5.0, -1.0 / 5.0, 8.0 / 315.0, -1.0 / 560.0)
 R = 4
+LANES = 128
+TOP = 32767.0
 MESH = pl.DeviceIdType.MESH
 
 
@@ -17,8 +19,8 @@
     n, nd,
     off_ref, img_hbm, bg_hbm, now_hbm, prev_hbm, cour_hbm,
     out_ref,
-    img, bg, wext, prev, cour, shift, acc, fin, part_out, part_in,
-    load_sem, img_sem, bg_send, bg_recv, halo_send, halo_recv, p_send, p_recv,
+    img, bg, wext, prev, cour, shift, acc, fin, part_out, part_in, scale_out, scale_in,
+    load_sem, img_sem, bg_send, bg_recv, halo_send, halo_recv, p_send, p_recv, s_send, s_recv,
 ):
     K, _, Z, X = img.shape
     Y = out_ref.shape[1]
@@ -136,15 +138,36 @@
 
         lax.fori_loop(0, K // group, body, 0)
 
-    def part_copy(j):
-        return pltpu.make_async_remote_copy(
-            src_ref=part_out.at[j], dst_ref=part_in.at[me], send_sem=p_send.at[j],
-            recv_sem=p_recv.at[me], device_id={"off": j}, device_id_type=MESH)
-
-    def part_arrival(j):
-        return pltpu.make_async_remote_copy(
-            src_ref=part_out.at[j], dst_ref=part_in.at[j], send_sem=p_send.at[j],
-            recv_sem=p_recv.at[j], device_id={"off": j}, device_id_type=MESH)
+    def fold(full):
+        top = jnp.max(full, axis=0)
+        rows8 = functools.reduce(jnp.maximum, [top[z : z + 8] for z in range(0, Z, 8)])
+        return functools.reduce(
+            jnp.maximum, [rows8[:, x : x + LANES] for x in range(0, X, LANES)])
+
+    def spread(small):
+        return jnp.concatenate(
+            [jnp.concatenate([small] * (X // LANES), axis=1)] * (Z // 8), axis=0)
+
+    def encode(j):
+        top = fold(jnp.abs(acc[1]))
+        scale_out[j] = top * (1.0 / TOP)
+        up = spread(jnp.where(top > 0.0, TOP / top, 0.0))
+        for y in range(Y):
+            whole = jnp.round(jnp.clip(acc[1, y] * up, -TOP, TOP)).astype(jnp.int32)
+            part_out[j, y] = whole.astype(jnp.int16)
+
+    def decoded(j):
+        down = spread(scale_in[j])
+        return part_in[j].astype(jnp.int32).astype(jnp.float32) * down[None]
+
+    def part_copies(j, slot):
+        return [
+            pltpu.make_async_remote_copy(
+                src_ref=src.at[j], dst_ref=dst.at[slot], send_sem=send.at[j],
+                recv_sem=recv.at[slot], device_id={"off": j}, device_id_type=MESH)
+            for src, dst, send, recv in (
+                (scale_out, scale_in, s_send, s_recv), (part_out, part_in, p_send, p_recv))
+        ]
 
     img_load(me).wait()
     partial(me, acc, 0)
@@ -165,8 +188,10 @@
             @pl.when(ok)
             def _():
                 img_load(j).wait()
-                partial(j, part_out, j)
-                part_copy(j).start()
+                partial(j, acc, 1)
+                encode(j)
+                for copy in part_copies(j, me):
+                    copy.start()
 
     ld_prev.wait()
     ld_cour.wait()
@@ -201,8 +226,9 @@
         for j, ok in ((me - t, me - t >= 0), (me + t, me + t < n)):
             @pl.when(ok)
             def _():
-                part_arrival(j).wait_recv()
-                fin[...] = fin[...] + cour[...] * part_in[j]
+                for copy in part_copies(j, j):
+                    copy.wait_recv()
+                fin[...] = fin[...] + cour[...] * decoded(j)
     out_ref[0] = fin[...]
 
     for slot, side in enumerate("lr"):
@@ -216,7 +242,8 @@
         ):
             @pl.when(ok)
             def _():
-                part_copy(j).wait_send()
+                for copy in part_copies(j, me):
+                    copy.wait_send()
 
                 @pl.when(onward)
                 def _():
@@ -227,7 +254,7 @@
     K, rows, Z, X = image.shape
     Y = wave_now.shape[1]
     f32 = jnp.float32
-    anywhere = pl.BlockSpec(memory_space=pl.ANY)
+    anywhere = pl.BlockSpec(memory_space=pltpu.HBM)
     dma = pltpu.SemaphoreType.DMA
     return pl.pallas_call(
         functools.partial(kernel, n, nd),
@@ -241,15 +268,17 @@
             pltpu.VMEM((Y, Z, X), f32),
             pltpu.VMEM((Y, Z, X), f32),
             pltpu.VMEM((K, X, X), jnp.bfloat16),
-            pltpu.VMEM((1, Y, Z, X), f32),
+            pltpu.VMEM((2, Y, Z, X), f32),
             pltpu.VMEM((Y, Z, X), f32),
-            pltpu.VMEM((n, Y, Z, X), f32),
-            pltpu.VMEM((n, Y, Z, X), f32),
+            pltpu.VMEM((n, Y, Z, X), jnp.int16),
+            pltpu.VMEM((n, Y, Z, X), jnp.int16),
+            pltpu.VMEM((n, 8, LANES), f32),
+            pltpu.VMEM((n, 8, LANES), f32),
             dma((4,)), dma((n,)), dma((2, n)), dma((n,)), dma((4,)), dma((4,)),
-            dma((n,)), dma((n,)),
+            dma((n,)), dma((n,)), dma((n,)), dma((n,)),
         ],
         compiler_params=pltpu.CompilerParams(
-            collective_id=0, has_side_effects=True, vmem_limit_bytes=48 * 2**20),
+            collective_id=0, has_side_effects=True, vmem_limit_bytes=67043328),
         name="born_step",
     )(offset_of, image, background, wave_now, wave_prev, courant)
 

time: 31.2 us -> 24.2 us (0.78)
  local copies, waits for them, and re-layouts: 7.05 us -> 1.57 us
  Pallas kernels: 23.9 us -> 22.5 us
    unnamed x13 -> x1, local copies, waits for them, and re-layouts: 7.05 us -> 1.57 us
    pallas_call x1, Pallas kernels: 23.9 us -> 22.5 us  [on_device(): pl.pallas_call(functools.partial(kernel, n, nd), out_shape=jax.ShapeDtype...]
where the time goes in v2:
time: 24.2 us; the launch traced here: 24.1 us
  Pallas kernels  22.5 us (93%)
  local copies, waits for them, and re-layouts  1.57 us (6%)
    pallas_call x1, Pallas kernels, on_device(): pl.pallas_call(functools.partial(kernel, n, nd), out_shape=jax.ShapeDtype...  22.5 us
    unnamed x1, local copies, waits for them, and re-layouts  1.57 us

profile of v2, /device:TPU:0, one launch (start us, length us, event | category | flops | bytes accessed | tf_op | source)
XLA Modules:
  0.0 24.1 jit_solution(13676539033987254373)
XLA Ops:
  0.0 22.5 %born_step.1 = f32[1,8,16,256]{3,2,1,0:T(8,128)} custom-call(s32[16]{0:T(128)} %off_ref.1, bf16[16,32,16,256]{3,2,1,0:T(8,128)(2,1)} %img_hbm.1, bf16[1,8,16,256]{3,2,1,0:T(8,128)(2,1)} %bg_hbm.1, f32[1,8,16,256]{3,2,1,0:T(8,128)} %now_hbm.1, f32[1,8,16,256]{3,2,1,0:T(8,128)} %prev_hbm.1, f32[8,16,256]{2,1,0:T(8,128)} %cour_hbm.1), custom_call_target="tpu_custom_call" | custom-call | tf_op jit(solution)/shard_map/born_step/pallas_call | solution.py:259
  22.5 1.6 %copy.8 = f32[1,8,16,256]{3,2,1,0:T(8,128)} copy(f32[1,8,16,256]{3,2,1,0:T(8,128)} %born_step.1) | data formatting | bytes 262144

commit v3 on v2

--- a/solution.py
+++ b/solution.py
@@ -12,6 +12,7 @@
 R = 4
 LANES = 128
 TOP = 32767.0
+PIECES = 2
 MESH = pl.DeviceIdType.MESH
 
 
@@ -19,7 +20,7 @@
     n, nd,
     off_ref, img_hbm, bg_hbm, now_hbm, prev_hbm, cour_hbm,
     out_ref,
-    img, bg, wext, prev, cour, shift, acc, fin, part_out, part_in, scale_out, scale_in,
+    img, bg, wext, prev, cour, shift, acc, part_out, part_in, scale_out, scale_in,
     load_sem, img_sem, bg_send, bg_recv, halo_send, halo_recv, p_send, p_recv, s_send, s_recv,
 ):
     K, _, Z, X = img.shape
@@ -30,6 +31,8 @@
     near = {"l": {"off": me - 1}, "r": {"off": me + 1},
             "u": {"depth": dep - 1}, "d": {"depth": dep + 1}}
 
+    fin = out_ref.at[0]
+
     own = wext.at[pl.ds(R, Y), pl.ds(8, Z), :]
     ld_bg = pltpu.make_async_copy(bg_hbm.at[0], bg.at[me], load_sem.at[0])
     ld_now = pltpu.make_async_copy(now_hbm.at[0], own, load_sem.at[1])
@@ -77,17 +80,21 @@
         shift[k] = jnp.where(lead == h, 1.0, 0.0).astype(jnp.bfloat16)
         return carry
 
-    half = K // 2
-    lax.fori_loop(0, half, build, 0)
+    lax.fori_loop(0, K, build, 0)
     ld_bg.wait()
     ld_now.wait()
     count = sum(has[s].astype(jnp.int32) for s in "lrud")
     pl.semaphore_wait(barrier, count)
 
-    def bg_copy(j, side, slot):
+    step = Y // PIECES if Y % PIECES == 0 else Y
+    pieces = Y // step
+
+    def bg_copy(j, c, target, slot):
+        block = bg.at[j, pl.ds(c * step, step)]
         return pltpu.make_async_remote_copy(
-            src_ref=bg.at[j], dst_ref=bg.at[j], send_sem=bg_send.at[slot, j],
-            recv_sem=bg_recv.at[j], device_id=near[side], device_id_type=MESH)
+            src_ref=block, dst_ref=block, send_sem=bg_send.at[slot, j * pieces + c],
+            recv_sem=bg_recv.at[j * pieces + c], device_id={"off": target},
+            device_id_type=MESH)
 
     mine = {"l": (pl.ds(R, R), pl.ds(8, Z)), "r": (pl.ds(Y, R), pl.ds(8, Z)),
             "u": (pl.ds(R, Y), pl.ds(8, 8)), "d": (pl.ds(R, Y), pl.ds(Z, 8))}
@@ -102,16 +109,16 @@
             send_sem=halo_send.at[num[side]], recv_sem=halo_recv.at[num[there]],
             device_id=near[side], device_id_type=MESH)
 
-    for slot, side in enumerate("lr"):
+    for c in range(pieces):
+        for slot, side in enumerate("lr"):
+            @pl.when(has[side])
+            def _():
+                bg_copy(me, c, near[side]["off"], slot).start()
+    for side in "ud":
         @pl.when(has[side])
         def _():
-            bg_copy(me, side, slot).start()
-    for side in "udlr":
-        @pl.when(has[side])
-        def _():
             halo_copy(side).start()
 
-    lax.fori_loop(half, K, build, 0)
 
     group = 4 if K % 4 == 0 else 1
 
@@ -169,29 +176,45 @@
                 (scale_out, scale_in, s_send, s_recv), (part_out, part_in, p_send, p_recv))
         ]
 
+    def arrivals(t):
+        return ((me - t, me - t >= 0, 1), (me + t, me + t < n, -1))
+
+    def onward(t, sign):
+        if t % 2 == 0:
+            return ()
+        spots = [(me + hop * sign, slot) for slot, hop in ((1, 2), (0, 1))]
+        return [(to, jnp.logical_and(to >= 0, to < n), slot) for to, slot in spots]
+
     img_load(me).wait()
     partial(me, acc, 0)
 
+    def send_partial(j, ok):
+        @pl.when(ok)
+        def _():
+            img_load(j).wait()
+            partial(j, acc, 1)
+            encode(j)
+            for copy in part_copies(j, me):
+                copy.start()
+
     for t in range(1, n):
-        for j, ok, onward, slot, side in (
-            (me - t, me - t >= 0, me < n - 1, 1, "r"),
-            (me + t, me + t < n, me > 0, 0, "l"),
-        ):
-            @pl.when(ok)
-            def _():
-                bg_copy(j, side, slot).wait_recv()
-
-                @pl.when(onward)
+        for c in range(pieces):
+            for j, ok, sign in arrivals(t):
+                @pl.when(ok)
                 def _():
-                    bg_copy(j, side, slot).start()
-        for j, ok in ((me - t, me - t >= 0), (me + t, me + t < n)):
-            @pl.when(ok)
-            def _():
-                img_load(j).wait()
-                partial(j, acc, 1)
-                encode(j)
-                for copy in part_copies(j, me):
-                    copy.start()
+                    bg_copy(j, c, me, 0).wait_recv()
+            for j, ok, sign in arrivals(t):
+                for to, there, slot in onward(t, sign):
+                    @pl.when(jnp.logical_and(ok, there))
+                    def _():
+                        bg_copy(j, c, to, slot).start()
+        if t == 1:
+            for side in "lr":
+                @pl.when(has[side])
+                def _():
+                    halo_copy(side).start()
+        for j, ok, sign in arrivals(t):
+            send_partial(j, ok)
 
     ld_prev.wait()
     ld_cour.wait()
@@ -229,25 +252,23 @@
                 for copy in part_copies(j, j):
                     copy.wait_recv()
                 fin[...] = fin[...] + cour[...] * decoded(j)
-    out_ref[0] = fin[...]
-
-    for slot, side in enumerate("lr"):
-        @pl.when(has[side])
-        def _():
-            bg_copy(me, side, slot).wait_send()
+
+    for c in range(pieces):
+        for slot, side in enumerate("lr"):
+            @pl.when(has[side])
+            def _():
+                bg_copy(me, c, near[side]["off"], slot).wait_send()
     for t in range(1, n):
-        for j, ok, onward, slot, side in (
-            (me - t, me - t >= 0, me < n - 1, 1, "r"),
-            (me + t, me + t < n, me > 0, 0, "l"),
-        ):
+        for j, ok, sign in arrivals(t):
             @pl.when(ok)
             def _():
                 for copy in part_copies(j, me):
                     copy.wait_send()
-
-                @pl.when(onward)
+            for to, there, slot in onward(t, sign):
+                @pl.when(jnp.logical_and(ok, there))
                 def _():
-                    bg_copy(j, side, slot).wait_send()
+                    for c in range(pieces):
+                        bg_copy(j, c, to, slot).wait_send()
 
 
 def on_device(n, nd, image, offset_of, background, wave_now, wave_prev, courant):
@@ -269,18 +290,18 @@
             pltpu.VMEM((Y, Z, X), f32),
             pltpu.VMEM((K, X, X), jnp.bfloat16),
             pltpu.VMEM((2, Y, Z, X), f32),
-            pltpu.VMEM((Y, Z, X), f32),
             pltpu.VMEM((n, Y, Z, X), jnp.int16),
             pltpu.VMEM((n, Y, Z, X), jnp.int16),
             pltpu.VMEM((n, 8, LANES), f32),
             pltpu.VMEM((n, 8, LANES), f32),
-            dma((4,)), dma((n,)), dma((2, n)), dma((n,)), dma((4,)), dma((4,)),
+            dma((4,)), dma((n,)), dma((2, n * PIECES)), dma((n * PIECES,)), dma((4,)), dma((4,)),
             dma((n,)), dma((n,)), dma((n,)), dma((n,)),
         ],
         compiler_params=pltpu.CompilerParams(
-            collective_id=0, has_side_effects=True, vmem_limit_bytes=67043328),
+            collective_id=0, has_side_effects=True, vmem_limit_bytes=50331648),
         name="born_step",
-    )(offset_of, image, background, wave_now, wave_prev, courant)
+    )(*[pltpu.with_memory_space_constraint(a, pltpu.HBM) for a in
+        (offset_of, image, background, wave_now, wave_prev, courant)])
 
 
 def solution(mesh):

time: 24.2 us -> 21.8 us (0.901)
  Pallas kernels: 22.5 us -> 21 us
  local copies, waits for them, and re-layouts: 1.57 us -> 0.66 us
    pallas_call x1, Pallas kernels: 22.5 us -> 21 us  [on_device(): pl.pallas_call(functools.partial(kernel, n, nd), out_shape=jax.ShapeDtype...]
    unnamed x1, local copies, waits for them, and re-layouts: 1.57 us -> 0.66 us
where the time goes in v3:
time: 21.8 us; the launch traced here: 21.7 us
  Pallas kernels  21 us (96%)
  local copies, waits for them, and re-layouts  0.66 us (3%)
    pallas_call x1, Pallas kernels, on_device(): pl.pallas_call(functools.partial(kernel, n, nd), out_shape=jax.ShapeDtype...  21 us
    unnamed x1, local copies, waits for them, and re-layouts  0.66 us

profile of v3, /device:TPU:0, one launch (start us, length us, event | category | flops | bytes accessed | tf_op | source)
XLA Modules:
  0.0 21.7 jit_solution(621103443439821192)
XLA Ops:
  0.0 21.0 %born_step.1 = f32[1,8,16,256]{3,2,1,0:T(8,128)S(1)} custom-call(s32[16]{0:T(128)} %off_ref.1, bf16[16,32,16,256]{3,2,1,0:T(8,128)(2,1)} %img_hbm.1, bf16[1,8,16,256]{3,2,1,0:T(8,128)(2,1)} %bg_hbm.1, f32[1,8,16,256]{3,2,1,0:T(8,128)} %now_hbm.1, f32[1,8,16,256]{3,2,1,0:T(8,128)} %prev_hbm.1, f32[8,16,256]{2,1,0:T(8,128)} %cour_hbm.1), custom_call_target="tpu_custom_call" | custom-call | tf_op jit(solution)/shard_map/born_step/pallas_call | solution.py:280
  21.0 0.7 %copy.8 = f32[1,8,16,256]{3,2,1,0:T(8,128)} copy(f32[1,8,16,256]{3,2,1,0:T(8,128)S(1)} %born_step.1) | data formatting | bytes 262144

commit v4 on v3

--- a/solution.py
+++ b/solution.py
@@ -12,7 +12,7 @@
 R = 4
 LANES = 128
 TOP = 32767.0
-PIECES = 2
+PIECES = 4
 MESH = pl.DeviceIdType.MESH
 
 
@@ -114,7 +114,7 @@
             @pl.when(has[side])
             def _():
                 bg_copy(me, c, near[side]["off"], slot).start()
-    for side in "ud":
+    for side in "lrud":
         @pl.when(has[side])
         def _():
             halo_copy(side).start()
@@ -197,7 +197,8 @@
             for copy in part_copies(j, me):
                 copy.start()
 
-    for t in range(1, n):
+    order = [1] + [t for low in range(2, n, 2) for t in (low + 1, low) if t < n]
+    for t in order:
         for c in range(pieces):
             for j, ok, sign in arrivals(t):
                 @pl.when(ok)
@@ -208,11 +209,6 @@
                     @pl.when(jnp.logical_and(ok, there))
                     def _():
                         bg_copy(j, c, to, slot).start()
-        if t == 1:
-            for side in "lr":
-                @pl.when(has[side])
-                def _():
-                    halo_copy(side).start()
         for j, ok, sign in arrivals(t):
             send_partial(j, ok)
 

time: 21.8 us -> 20.9 us (0.959)
  Pallas kernels: 21 us -> 20.1 us
    pallas_call x1, Pallas kernels: 21 us -> 20.1 us  [on_device(): pl.pallas_call(functools.partial(kernel, n, nd), out_shape=jax.ShapeDtype...]
where the time goes in v4:
time: 20.9 us; the launch traced here: 20.7 us
  Pallas kernels  20.1 us (96%)
  local copies, waits for them, and re-layouts  0.66 us (3%)
    pallas_call x1, Pallas kernels, on_device(): pl.pallas_call(functools.partial(kernel, n, nd), out_shape=jax.ShapeDtype...  20.1 us
    unnamed x1, local copies, waits for them, and re-layouts  0.66 us

profile of v4, /device:TPU:0, one launch (start us, length us, event | category | flops | bytes accessed | tf_op | source)
XLA Modules:
  0.0 20.7 jit_solution(4187095327269337599)
XLA Ops:
  0.0 20.1 %born_step.1 = f32[1,8,16,256]{3,2,1,0:T(8,128)S(1)} custom-call(s32[16]{0:T(128)} %off_ref.1, bf16[16,32,16,256]{3,2,1,0:T(8,128)(2,1)} %img_hbm.1, bf16[1,8,16,256]{3,2,1,0:T(8,128)(2,1)} %bg_hbm.1, f32[1,8,16,256]{3,2,1,0:T(8,128)} %now_hbm.1, f32[1,8,16,256]{3,2,1,0:T(8,128)} %prev_hbm.1, f32[8,16,256]{2,1,0:T(8,128)} %cour_hbm.1), custom_call_target="tpu_custom_call" | custom-call | tf_op jit(solution)/shard_map/born_step/pallas_call | solution.py:276
  20.1 0.7 %copy.8 = f32[1,8,16,256]{3,2,1,0:T(8,128)} copy(f32[1,8,16,256]{3,2,1,0:T(8,128)S(1)} %born_step.1) | data formatting | bytes 262144
